TPU v7x, 128 devices: a whole 4x4x4 slice. The times are simulated.
128 devices in a mesh: row: 8 (over x, core), col: 16 (over z, y).
Axes of the slice: x: 4, y: 4, z: 4, core: 2. Of those that a mesh axis runs over, the one named last changes fastest.
Arguments:
- embeddings: bfloat16 [32768, 1024], P(('row', 'col')), may hold values from -6 to 6
- features: bfloat16 [32768, 256], P(('row', 'col')), may hold values from -6 to 6
- candidates: int32 [256, 38], P(('row', 'col')), may hold values from 0 to 255, as said below
Outputs:
- smoothed: bfloat16 [32768, 256], P(('row', 'col'))
Inputs may be any that keep to these rules, and one draw needn't show every extreme that they name: `candidates`: each row names 38 distinct blocks. Over the blocks held by one row of devices, the entries that name blocks held by one column of devices number at most 160, and in every row of devices some column reaches that number.
All inputs are finite; a program needn't handle non-finite values.
Results may differ from a plain program's by a relative error of at most 0.012.
The roundings to bfloat16 on the way count: a program that leaves them out, or rounds other values in their place, can miss the bound.
Values may be sent and summed in bfloat16 or wider, within the bound.
No kernel may reach another device: no remote copies, remote signals or barrier semaphores. Data moves between devices by JAX's collectives and lax.ppermute only.
A program may use at most 128 MiB of HBM per device.

v0:
```python
import jax
import jax.numpy as jnp
from jax import lax
from jax.sharding import PartitionSpec as P

EMB = 1024
FEAT = 256
BLOCK = 128
NB_DEV = 2
BETA = 16


def unit_rows(embeddings):
    values = embeddings.astype(jnp.float32)
    factor = lax.rsqrt(jnp.mean(values * values, axis=1, keepdims=True) + 1e-06) * values.shape[
        1
    ] ** (-0.5)
    return (values * factor).astype(jnp.bfloat16)


def pair_lists(keep, cand_local, query_ids, block_lists):
    query_blocks, list_len = keep.shape
    kept_int = keep.astype(jnp.int32)
    rank = jnp.cumsum(kept_int, axis=1) - 1
    destination = jnp.where(keep, rank, list_len)
    query_rows = jnp.broadcast_to(
        jnp.arange(query_blocks, dtype=jnp.int32)[:, None], (query_blocks, list_len)
    )
    same_flag = (block_lists == query_ids[:, None]).astype(jnp.int32)
    blank_table = jnp.zeros((query_blocks, list_len), jnp.int32)
    cand_sel = blank_table.at[query_rows, destination].set(cand_local, mode="drop")
    same_sel = blank_table.at[query_rows, destination].set(same_flag, mode="drop")
    counts = jnp.sum(kept_int, axis=1)
    return (cand_sel, same_sel, counts)


def smooth_tile(query_units, cand_units, cand_feats, cand_sel, same_sel, counts):
    query_blocks, block_len, _ = query_units.shape
    feat_width = cand_feats.shape[2]
    diagonal_mask = jnp.eye(block_len, dtype=jnp.bool_)

    def turn(slot, state):
        numerator, denominator = state
        cand_idx = lax.dynamic_slice_in_dim(cand_sel, slot, 1, 1)[:, 0]
        same_idx = lax.dynamic_slice_in_dim(same_sel, slot, 1, 1)[:, 0]
        active = (slot < counts).astype(jnp.float32)
        cand_blk = jnp.take(cand_units, cand_idx, axis=0)
        feat_blk = jnp.take(cand_feats, cand_idx, axis=0)
        cosine = jnp.einsum(
            "qie,qje->qij", query_units, cand_blk, preferred_element_type=jnp.float32
        )
        weight = jnp.exp(BETA * (cosine - 1.0))
        is_self = jnp.logical_and(same_idx[:, None, None] > 0, diagonal_mask[None])
        weight = jnp.where(is_self, jnp.float32(0.0), weight) * active[:, None, None]
        numerator = numerator + jnp.einsum(
            "qij,qjf->qif",
            weight.astype(jnp.bfloat16),
            feat_blk,
            preferred_element_type=jnp.float32,
        )
        denominator = denominator + jnp.sum(weight, axis=2)
        return (numerator, denominator)

    turn_count = jnp.max(counts)
    initial = (
        jnp.zeros((query_blocks, block_len, feat_width), jnp.float32),
        jnp.zeros((query_blocks, block_len), jnp.float32),
    )
    return lax.fori_loop(0, turn_count, turn, initial)


def on_device(embeddings, features, candidates):
    units = unit_rows(embeddings)
    row_index = lax.axis_index("row")
    col_index = lax.axis_index("col")
    col_count = lax.axis_size("col")
    query_flat = lax.all_gather(units, "col", axis=0, tiled=True)
    block_lists = lax.all_gather(candidates, "col", axis=0, tiled=True)
    cand_flat, feat_flat = (
        lax.all_gather(units, "row", axis=0, tiled=True),
        lax.all_gather(features, "row", axis=0, tiled=True),
    )
    query_blocks = block_lists.shape[0]
    local = jnp.arange(query_blocks, dtype=jnp.int32)
    query_ids = (row_index * col_count + local // NB_DEV) * NB_DEV + local % NB_DEV
    holder = block_lists // NB_DEV
    keep = holder % col_count == col_index
    cand_local = holder // col_count * NB_DEV + block_lists % NB_DEV
    query_units = query_flat.reshape(-1, BLOCK, EMB)
    cand_units = cand_flat.reshape(-1, BLOCK, EMB)
    cand_feats = feat_flat.reshape(-1, BLOCK, FEAT)
    cand_sel, same_sel, counts = pair_lists(keep, cand_local, query_ids, block_lists)
    numerator, denominator = smooth_tile(
        query_units, cand_units, cand_feats, cand_sel, same_sel, counts
    )
    numerator, denominator = (
        lax.psum_scatter(numerator.reshape(-1, FEAT), "col", scatter_dimension=0, tiled=True),
        lax.psum_scatter(denominator.reshape(-1), "col", scatter_dimension=0, tiled=True),
    )
    return (numerator / denominator[:, None]).astype(jnp.bfloat16)


def solution(mesh):
    in_specs = (P(("row", "col"), None), P(("row", "col"), None), P(("row", "col"), None))
    out_specs = P(("row", "col"), None)
    return jax.shard_map(
        on_device, mesh=mesh, in_specs=in_specs, out_specs=out_specs, check_vma=False
    )
```

profile of v0, /device:TPU:0, one launch (start us, length us, event | category | flops | bytes accessed | tf_op | source)
XLA Modules:
  0.0 415.8 jit_solution(14212562513498291968)
XLA Ops:
  6.5 0.7 all-gather.9.cloned.1.call-update
  7.3 1.2 fusion.15
  8.5 2.0 fusion.16
  10.6 0.7 all-gather.7.cloned.1.call-update
  11.3 25.0 %all-gather = s32[16,2,38]{2,1,0:T(2,128)S(1)} all-gather(s32[1,2,38]{2,1,0:T(2,128)} %bitcast.38), channel_id=1, replica_groups=mesh['row'=8,'col'=16] {'col'}, dimensions={0}, use_global_device_ids=true | all-gather | bytes 5168 | tf_op jit(solution)/shard_map/all_gather | solution.py:78
  36.4 0.2 reduce_window_sum.11
  36.6 0.1 fusion.20
  36.7 0.7 multiply_reduce_fusion
  37.5 0.7 and_reduce_fusion
  38.2 0.1 reshape.115
  38.3 0.1 reshape.117
  38.4 6.4 %scatter_custom_fusion = s32[1216]{0:T(1024)S(1)} fusion(s32[1216]{0:T(1024)S(1)} %reshape.115, s32[1216]{0:T(1024)S(1)} %reshape.117, s32[]{:T(128)} %constant.154.clone.1), kind=kCustom, calls=%fused_computation.58 | custom fusion | bytes 4868
  45.1 0.1 reshape.123
  45.2 6.4 %scatter_custom_fusion.1 = s32[1216]{0:T(1024)S(1)} fusion(s32[1216]{0:T(1024)S(1)} %reshape.115, s32[1216]{0:T(1024)S(1)} %reshape.123, s32[]{:T(128)} %constant.154.clone.1), kind=kCustom, calls=%fused_computation.56 | custom fusion | bytes 4868
  51.8 0.7 reduce_max.9
  52.5 15.9 %all-gather.5.cloned.1.call-done = bf16[2048,1024]{1,0:T(8,128)(2,1)} async-done(((bf16[256,1024]{1,0:T(8,128)(2,1)}), bf16[2048,1024]{1,0:T(8,128)(2,1)}) %all-gather.5.cloned.1.call-update) | async-done | bytes 4194320 | tf_op jit(solution)/shard_map/all_gather | solution.py:80
  68.4 73.1 %all-gather.7.cloned.1.call-done = bf16[4096,1024]{1,0:T(8,128)(2,1)} async-done(((bf16[256,1024]{1,0:T(8,128)(2,1)}), bf16[4096,1024]{1,0:T(8,128)(2,1)}) %all-gather.7.cloned.1.call-update) | async-done | bytes 8388624 | tf_op jit(solution)/shard_map/all_gather | solution.py:77
  141.5 2.5 broadcast_in_dim.66
  144.0 47.3 %while.15 = (s32[]{:T(128)}, f32[32,128,256]{2,1,0:T(8,128)}, f32[32,128]{1,0:T(8,128)S(1)}, s32[]{:T(128)}, s32[32,38]{0,1:T(8,128)S(1)}, /*index=5*/s32[32,38]...) while((s32[]{:T(128)}, f32[32,128,256]{2,1,0:T(8,128)}, ...), condition=%wide.region_8.9_spmd.clone, body=%wide.region_6.8_spmd.clone.sunk | while | flops 1352156416 | bytes 50435528 | solution.py:69
  144.7 7.2 %gather_fusion.1 = bf16[32,128,1024]{2,1,0:T(8,128)(2,1)} fusion(bf16[16,128,1024]{2,1,0:T(8,128)(2,1)} %get-tuple-element.324, s32[1024]{0:T(1024)S(1)} %pad_clamp_fusion.2), kind=kCustom, calls=%fused_computation.clone.clone.1 | custom fusion | bytes 16777344 | tf_op jit(solution)/shard_map/while/body/jit(_take)/gather | solution.py:47
  152.0 9.3 %fusion.44 = (f32[32,128]{1,0:T(8,128)S(1)}, bf16[32,128,128]{1,2,0:T(8,128)(2,1)}) fusion(f32[32]{0:T(128)S(1)} %compare_convert_fusion.3, bf16[32,128,1024]{2,1,0:T(8,128)(2,1)} %get-tuple-element.325, bf16[32,128,1024]{2,1,0:T(8,128)(2,1)} %gather_fusion.1, pred[32]{0:T(512)(128)(4,1)S(1)} %get-tuple-element.289, ...), kind=kOutput, calls=%fused_computation.70.clone.1 | convolution fusion | flops 1081602048 | bytes 17858752 | tf_op jit(solution)/shard_map/while/body/qie,qje->qij/dot_general | solution.py:49
  161.3 0.7 gather_fusion
  162.0 5.3 %convolution_add_fusion.2 = f32[32,128,256]{2,1,0:T(8,128)} fusion(f32[32,128,256]{2,1,0:T(8,128)} %get-tuple-element.306, bf16[32,128,256]{2,1,0:T(8,128)(2,1)S(1)} %gather_fusion, pred[32]{0:T(512)(128)(4,1)S(1)} %get-tuple-element.289, bf16[32,128,128]{1,2,0:T(8,128)(2,1)} %get-tuple-element.290), kind=kOutput, calls=%fused_computation.9.clone.1 | convolution fusion | flops 270532608 | bytes 11534368 | tf_op jit(solution)/shard_map/while/body/qij,qjf->qif/dot_general | solution.py:55
  168.0 7.2 %gather_fusion.1 = bf16[32,128,1024]{2,1,0:T(8,128)(2,1)} fusion(bf16[16,128,1024]{2,1,0:T(8,128)(2,1)} %get-tuple-element.324, s32[1024]{0:T(1024)S(1)} %pad_clamp_fusion.2), kind=kCustom, calls=%fused_computation.clone.clone.1 | custom fusion | bytes 16777344 | tf_op jit(solution)/shard_map/while/body/jit(_take)/gather | solution.py:47
  175.3 9.3 %fusion.44 = (f32[32,128]{1,0:T(8,128)S(1)}, bf16[32,128,128]{1,2,0:T(8,128)(2,1)}) fusion(f32[32]{0:T(128)S(1)} %compare_convert_fusion.3, bf16[32,128,1024]{2,1,0:T(8,128)(2,1)} %get-tuple-element.325, bf16[32,128,1024]{2,1,0:T(8,128)(2,1)} %gather_fusion.1, pred[32]{0:T(512)(128)(4,1)S(1)} %get-tuple-element.289, ...), kind=kOutput, calls=%fused_computation.70.clone.1 | convolution fusion | flops 1081602048 | bytes 17858752 | tf_op jit(solution)/shard_map/while/body/qie,qje->qij/dot_general | solution.py:49
  184.6 0.7 gather_fusion
  185.3 5.3 %convolution_add_fusion.2 = f32[32,128,256]{2,1,0:T(8,128)} fusion(f32[32,128,256]{2,1,0:T(8,128)} %get-tuple-element.306, bf16[32,128,256]{2,1,0:T(8,128)(2,1)S(1)} %gather_fusion, pred[32]{0:T(512)(128)(4,1)S(1)} %get-tuple-element.289, bf16[32,128,128]{1,2,0:T(8,128)(2,1)} %get-tuple-element.290), kind=kOutput, calls=%fused_computation.9.clone.1 | convolution fusion | flops 270532608 | bytes 11534368 | tf_op jit(solution)/shard_map/while/body/qij,qjf->qif/dot_general | solution.py:55
  191.3 0.6 copy-done.1
  191.9 0.6 dynamic-slice
  193.2 203.6 %all-reduce = f32[4096]{0:T(1024)S(1)} all-reduce(f32[4096]{0:T(1024)S(1)} %bitcast.34), channel_id=3, replica_groups=mesh['row'=8,'col'=16] {'col'}, use_global_device_ids=true, to_apply=%region_10.11.clone | all-reduce | flops 4096 | bytes 32768
  396.8 10.7 %reduce-scatter.2.cloned.1.call-done = f32[256,256]{1,0:T(8,128)} async-done(((f32[4096,256]{1,0:T(8,128)}), f32[256,256]{1,0:T(8,128)}) %reduce-scatter.2.cloned.1.call-update) | async-done | bytes 262160 | tf_op jit(solution)/shard_map/reduce_scatter | solution.py:97
  407.5 1.7 divide_convert_fusion
  (34 shorter events, 0.9 us)
Async XLA Ops:
  6.5 46.0 %all-gather.9.cloned.1.call-start = ((), (), s32[]{:S(2)}) async-start(), calls=%async_computation.3 | async-start | bytes 1179648 | tf_op jit(solution)/shard_map/all_gather | solution.py:81
  7.3 61.2 %all-gather.5.cloned.1.call-start = ((), (), s32[]{:S(2)}) async-start(), calls=%async_computation.1 | async-start | bytes 4718592 | tf_op jit(solution)/shard_map/all_gather | solution.py:80
  10.6 131.0 %all-gather.7.cloned.1.call-start = ((), (), s32[]{:S(2)}) async-start(), calls=%async_computation.2 | async-start | bytes 8912896 | tf_op jit(solution)/shard_map/all_gather | solution.py:77
  11.3 396.2 %reduce-scatter.2.cloned.1.call-start = ((), (), s32[]{:S(2)}) async-start(), calls=%async_computation.4 | async-start | bytes 4456448 | tf_op jit(solution)/shard_map/reduce_scatter | solution.py:97
  52.5 91.5 %copy-start = (bf16[2048,256]{1,0:T(8,128)(2,1)S(1)}, bf16[2048,256]{1,0:T(8,128)(2,1)}, u32[]{:S(2)}) copy-start(bf16[2048,256]{1,0:T(8,128)(2,1)} %all-gather.9.cloned.1.call-done) | copy-start | bytes 3145732
  191.3 0.7 copy-start.1
Sparse Core Ops, SparseCore 0:
  9.0 25.6 all-gather.8
  36.5 31.9 all-gather.4
  70.6 70.8 all-gather.6
  191.4 216.0 reduce-scatter.1
where the time goes:
time: 417 us; the launch traced here: 416 us
  blocking collectives  229 us (55%)
  waiting for transfers between devices  101 us (24%)
  local copies, waits for them, and re-layouts  33 us (8%)
  matrix products  29.2 us (7%)
  between operations  13.9 us (3%)
  other arithmetic  7.67 us (2%)
    unnamed x1, blocking collectives  204 us
    all_gather x1, waiting for transfers between devices, on_device(): query_flat = lax.all_gather(units, 'col', axis=0, tiled=True)  73.1 us
    all_gather x1, blocking collectives, on_device(): block_lists = lax.all_gather(candidates, 'col', axis=0, tiled=True)  25 us
    dot_general x2, matrix products, turn(): jnp.einsum('qie,qje->qij', query_units, cand_blk, preferred_element_type=...  18.6 us
    all_gather x1, waiting for transfers between devices, on_device(): lax.all_gather(units, 'row', axis=0, tiled=True)  15.9 us
    unnamed x11, local copies, waits for them, and re-layouts  14.4 us
    gather x2, local copies, waits for them, and re-layouts, turn(): cand_blk = jnp.take(cand_units, cand_idx, axis=0)  14.4 us
    reduce_scatter x1, waiting for transfers between devices, on_device(): lax.psum_scatter(numerator.reshape(-1, FEAT), 'col', scatter_dimension=0,...  10.7 us
  transfers between devices with their start and end apart: 4, of which 3 were waited for; matrix products, arithmetic and copies ran while one was open for 5% of the time, Pallas kernels for 0%

commit v1 on v0

v1 whole, which is shorter than its diff:
```python
import functools

import jax
import jax.numpy as jnp
from jax import lax
from jax.experimental import pallas as pl
from jax.experimental.pallas import tpu as pltpu
from jax.sharding import PartitionSpec as P


EMB = 1024
FEAT = 256
BLOCK = 128
NB_DEV = 2
BETA = 16
DOCS_DEV = NB_DEV * BLOCK
LIST_ROWS = 16
AXES = ("row", "col")
VALID, SELF = 1 << 11, 1 << 10


def hop(dx=0, dz=0, flip_core=False, y_of=lambda y: y):
    pairs = []
    for x in range(4):
        for k in range(2):
            for z in range(4):
                for y in range(4):
                    x2, k2, z2, y2 = (x + dx) % 4, (1 - k if flip_core else k), (z + dz) % 4, y_of(y)
                    pairs.append(((2 * x + k) * 16 + 4 * z + y, (2 * x2 + k2) * 16 + 4 * z2 + y2))
    return pairs


def partner_a(y):
    return y ^ 1


def partner_b(y):
    return 3 - y


def send(value, **where):
    return lax.ppermute(value, AXES, hop(**where))


def cand_kernel(emb_ref, feat_ref, cand_ref):
    values = emb_ref[...].astype(jnp.float32)
    factor = lax.rsqrt(jnp.mean(values * values, axis=1, keepdims=True) + 1e-06) * EMB ** (-0.5)
    cand_ref[:, pl.ds(0, EMB)] = (values * factor).astype(jnp.bfloat16)
    cand_ref[:, pl.ds(EMB, FEAT)] = feat_ref[...]


def query_kernel(unit_ref, own_ref, partner_ref, query_ref):
    query_ref[pl.ds(0, DOCS_DEV), :] = unit_ref[...]
    query_ref[pl.ds(DOCS_DEV, LIST_ROWS), :] = jnp.zeros((LIST_ROWS, EMB), jnp.bfloat16)
    for lane, ref in ((0, own_ref), (BLOCK, partner_ref)):
        lists, length = ref.shape
        query_ref[pl.ds(DOCS_DEV, lists), pl.ds(lane, length)] = (
            ref[...].astype(jnp.float32).astype(jnp.bfloat16)
        )


def small(limit=8):
    return pltpu.CompilerParams(vmem_limit_bytes=limit << 20)


def cand_payload(embeddings, features):
    return pl.pallas_call(
        cand_kernel,
        out_shape=jax.ShapeDtypeStruct((DOCS_DEV, EMB + FEAT), jnp.bfloat16),
        name="cand",
    )(embeddings, features)


def query_payload(cand, own, partner):
    return pl.pallas_call(
        query_kernel,
        grid=(1,),
        in_specs=[
            pl.BlockSpec((DOCS_DEV, EMB), lambda i: (0, 0)),
            pl.BlockSpec(own.shape, lambda i: (0, 0)),
            pl.BlockSpec(partner.shape, lambda i: (0, 0)),
        ],
        out_specs=pl.BlockSpec((DOCS_DEV + LIST_ROWS, EMB), lambda i: (0, 0)),
        out_shape=jax.ShapeDtypeStruct((DOCS_DEV + LIST_ROWS, EMB), jnp.bfloat16),
        name="query",
    )(cand, own, partner)


Q_FROM = ((0, 0), (-1, 0), (1, 0), (0, 1), (2, 0), (-1, 1), (1, 1), (2, 1))
LATE_FROM, EARLY_FROM = ((-1, 1), (1, 1)), ((0, 0), (0, 1), (2, 0), (-1, 0), (1, 0), (2, 1))
C_FROM = tuple((core, *f) for group in (LATE_FROM, EARLY_FROM) for core in (0, 1) for f in group)
Q_EARLY = 5
N_LATE, N_EARLY = 2 * len(LATE_FROM), 2 * len(EARLY_FROM)
SLOTS, COUNT = 384, 376


def codes_kernel(own_ref, partner_ref, r_ref, l_ref, o_ref, out_ref, stage, lists, sems):
    copies = [
        pltpu.make_async_copy(ref.at[pl.ds(DOCS_DEV, LIST_ROWS), pl.ds(0, 2 * BLOCK)], stage.at[i], sems.at[i])
        for i, ref in enumerate((r_ref, l_ref, o_ref))
    ]
    for copy in copies:
        copy.start()
    length = own_ref.shape[1]
    lists[...] = jnp.full_like(lists, -1.0)
    lists[pl.ds(0, 2), pl.ds(0, length)] = own_ref[...].astype(jnp.float32)
    lists[pl.ds(6, 2), pl.ds(0, length)] = partner_ref[...].astype(jnp.float32)
    for copy in copies:
        copy.wait()
    for i, (own_at, partner_at) in enumerate(((2, 10), (4, 12), (8, 14))):
        values = stage[i].astype(jnp.float32)
        lists[pl.ds(own_at, 2), pl.ds(0, length)] = values[0:2, 0:length]
        lists[pl.ds(partner_at, 2), pl.ds(0, length)] = values[0:2, BLOCK : BLOCK + length]
    named = lists[...]
    queries = named.shape[0]

    row, col = lax.axis_index("row"), lax.axis_index("col")
    x, k, z, y = row >> 1, row & 1, col >> 2, col & 3
    lane = lax.broadcasted_iota(jnp.int32, (1, BLOCK), 1)
    ids = jnp.full((1, BLOCK), -2, jnp.int32)
    for i, (core, dz, partner) in enumerate(C_FROM):
        yy = 3 - y if partner else y
        kk = 1 - k if core else k
        device = (2 * x + kk) * 16 + ((z + dz) & 3) * 4 + yy
        ids = jnp.where((lane >> 1) == i, device * NB_DEV + (lane & 1), ids)

    blocks = lax.broadcasted_iota(jnp.int32, (queries, 256), 1).astype(jnp.float32)
    onehot = jnp.zeros((queries, 256), jnp.float32)
    for i in range(length):
        onehot = jnp.where(named[:, i : i + 1] == blocks, 1.0, onehot)
    chosen = jnp.where(lax.broadcasted_iota(jnp.int32, (256, BLOCK), 0) == ids, 1.0, 0.0)
    member = jnp.dot(
        onehot.astype(jnp.bfloat16), chosen.astype(jnp.bfloat16), preferred_element_type=jnp.float32
    )
    ahead = jnp.where(
        lax.broadcasted_iota(jnp.int32, (BLOCK, BLOCK), 0) < lax.broadcasted_iota(jnp.int32, (BLOCK, BLOCK), 1),
        1.0,
        0.0,
    ).astype(jnp.bfloat16)
    above = jnp.where(
        lax.broadcasted_iota(jnp.int32, (queries, queries), 0)
        > lax.broadcasted_iota(jnp.int32, (queries, queries), 1),
        1.0,
        0.0,
    ).astype(jnp.bfloat16)
    query = lax.broadcasted_iota(jnp.int32, (queries, BLOCK), 0)
    cand = lax.broadcasted_iota(jnp.int32, (queries, BLOCK), 1)
    old_query = query < Q_EARLY * NB_DEV
    late_end, half = N_LATE * NB_DEV, (N_LATE + N_EARLY // 2) * NB_DEV
    first_half = jnp.logical_and(cand >= late_end, cand < half)
    calls = (
        (jnp.logical_and(old_query, first_half), jnp.logical_and(old_query, cand >= half)),
        (cand < late_end, jnp.logical_and(jnp.logical_not(old_query), cand >= late_end)),
    )
    slot = lax.broadcasted_iota(jnp.int32, (1, SLOTS), 1)
    slots = slot.astype(jnp.float32)
    places = (N_LATE + N_EARLY) * NB_DEV
    place = lax.broadcasted_iota(jnp.int32, (places, 1), 0)
    for call, groups in enumerate(calls):
        base = jnp.zeros((1, 1), jnp.float32)
        position = jnp.full((queries, BLOCK), -1.0, jnp.float32)
        totals = []
        for group in groups:
            inside = jnp.where(group, member, 0.0)
            bits = inside.astype(jnp.bfloat16)
            in_row = jnp.dot(bits, ahead, preferred_element_type=jnp.float32)
            rows_above = jnp.sum(
                jnp.dot(above, bits, preferred_element_type=jnp.float32), axis=1, keepdims=True
            )
            position = jnp.where(inside > 0.0, base + rows_above + in_row, position)
            base = base + jnp.sum(jnp.sum(inside, axis=1, keepdims=True), axis=0, keepdims=True)
            totals.append(base)
        by_cand = jnp.concatenate(
            [position, jnp.full((BLOCK - queries, BLOCK), -1.0, jnp.float32)], axis=0
        ).T
        found = jnp.zeros((places, SLOTS), jnp.float32)
        first_place = 0 if call else late_end
        for q in range(queries):
            code = q + 32 * (place - first_place) + VALID
            if q < NB_DEV:
                code = code + jnp.where(place == late_end + q, SELF, 0)
            found = jnp.where(by_cand[0:places, q : q + 1] == slots, code.astype(jnp.float32), found)
        line = jnp.sum(found, axis=0, keepdims=True)
        line = jnp.where(slot == COUNT, totals[1], jnp.where(slot == COUNT + 1, totals[0], line))
        out_ref[pl.ds(call, 1), :] = line.astype(jnp.int32)


def pair_codes(own, partner, q_r, q_l, q_o):
    free, vmem = pl.BlockSpec(memory_space=pl.ANY), pl.BlockSpec(memory_space=pltpu.VMEM)
    return pl.pallas_call(
        codes_kernel,
        in_specs=[vmem, vmem, free, free, free],
        out_specs=vmem,
        out_shape=jax.ShapeDtypeStruct((2, SLOTS), jnp.int32),
        scratch_shapes=[
            pltpu.VMEM((3, LIST_ROWS, 2 * BLOCK), jnp.bfloat16),
            pltpu.VMEM((len(Q_FROM) * NB_DEV, BLOCK), jnp.float32),
            pltpu.SemaphoreType.DMA((3,)),
        ],
        compiler_params=small(),
        name="codes",
    )(own, partner, q_r, q_l, q_o)


UNROLL = 8
QUERIES = 8


def smooth_kernel(nq, nc, own, first_cands, last, *refs):
    codes = refs[0]
    q_in, c_in = refs[1 : 1 + nq], refs[1 + nq : 1 + nq + nc]
    num, den, q_buf, c_buf, sems = refs[-5:]
    state = refs[1 + nq + nc : 3 + nq + nc]
    old = state[0].shape[0]
    copies = []

    def load(source, target):
        copies.append(pltpu.make_async_copy(source, target, sems.at[len(copies)]))
        copies[-1].start()

    load(c_in[own].at[:, pl.ds(0, EMB)], q_buf.at[pl.ds(0, DOCS_DEV), :])
    for i, ref in enumerate(q_in):
        load(ref.at[pl.ds(0, DOCS_DEV), :], q_buf.at[pl.ds((i + 1) * DOCS_DEV, DOCS_DEV), :])
    if last:
        load(state[0], num.at[pl.ds(0, old), :])
        load(state[1], den.at[pl.ds(0, old), :])
    for i, ref in enumerate(c_in):
        load(ref, c_buf.at[pl.ds(i * DOCS_DEV, DOCS_DEV), :])
    fresh = pl.ds(old, num.shape[0] - old) if last else pl.ds(0, old)
    num[fresh, :] = jnp.zeros((fresh.size, FEAT), jnp.float32)
    den[fresh, :] = jnp.zeros((fresh.size, BLOCK), jnp.float32)
    waited = len(copies) - nc + first_cands
    for copy in copies[:waited]:
        copy.wait()
    diagonal = lax.broadcasted_iota(jnp.int32, (BLOCK, BLOCK), 0) == lax.broadcasted_iota(
        jnp.int32, (BLOCK, BLOCK), 1
    )
    call = 1 if last else 0

    def turn(i, carry):
        pairs = []
        for u in range(UNROLL):
            code = codes[call, i * UNROLL + u]
            at_q = pl.ds(pl.multiple_of((code & 31) * BLOCK, BLOCK), BLOCK)
            at_c = pl.ds(pl.multiple_of(((code >> 5) & 31) * BLOCK, BLOCK), BLOCK)
            pairs.append((code, at_q, at_c))
        cosines = [
            lax.dot_general(
                q_buf[at_q, :],
                c_buf[at_c, pl.ds(0, EMB)],
                (((1,), (1,)), ((), ())),
                preferred_element_type=jnp.float32,
            )
            for _, at_q, at_c in pairs
        ]
        weights = []
        for (code, _, _), cosine in zip(pairs, cosines):
            weight = jnp.exp(BETA * (cosine - 1.0))
            drop = jnp.logical_or(code < VALID, jnp.logical_and((code & SELF) > 0, diagonal))
            weights.append(jnp.where(drop, 0.0, weight))
        terms = [
            jnp.dot(
                weight.astype(jnp.bfloat16),
                c_buf[at_c, pl.ds(EMB, FEAT)],
                preferred_element_type=jnp.float32,
            )
            for (_, _, at_c), weight in zip(pairs, weights)
        ]
        for (_, at_q, _), weight, term in zip(pairs, weights, terms):
            den[at_q, :] += weight
            num[at_q, :] += term
        return carry

    ready = codes[call, COUNT + 1] // UNROLL
    lax.fori_loop(0, ready, turn, 0)
    for copy in copies[waited:]:
        copy.wait()
    lax.fori_loop(ready, (codes[call, COUNT] + UNROLL - 1) // UNROLL, turn, 0)
    if not last:
        for i, (source, target) in enumerate(((num, state[0]), (den, state[1]))):
            pltpu.make_async_copy(source, target, sems.at[i]).start()
        for i, (source, target) in enumerate(((num, state[0]), (den, state[1]))):
            pltpu.make_async_copy(source, target, sems.at[i]).wait()
        return
    payloads = refs[3 + nq + nc : -5]
    ones = jnp.ones((8, BLOCK), jnp.bfloat16)

    def lane_sums(part):
        return lax.dot_general(ones, part, (((1,), (1,)), ((), ())), preferred_element_type=jnp.float32)

    for i, payload in enumerate(payloads):
        docs = pl.ds(i * DOCS_DEV, DOCS_DEV)
        payload[pl.ds(0, DOCS_DEV), :] = num[docs, :].astype(jnp.bfloat16)
        weights = den[docs, :]
        high = weights.astype(jnp.bfloat16)
        middle = (weights - high.astype(jnp.float32)).astype(jnp.bfloat16)
        sums = lane_sums(high) + lane_sums(middle)
        high = sums.astype(jnp.bfloat16).astype(jnp.float32)
        pair = jnp.concatenate([high, sums - high], axis=0).astype(jnp.bfloat16)
        payload[pl.ds(DOCS_DEV, 16), :] = pair


def smooth(codes, queries, cands, own, first_cands, state):
    docs, last = (1 + len(queries)) * DOCS_DEV, state is not None
    free, hbm, vmem, smem = (
        pl.BlockSpec(memory_space=space) for space in (pl.ANY, pltpu.HBM, pltpu.VMEM, pltpu.SMEM)
    )
    operands = [codes, *queries, *cands, *(state or ())]
    if last:
        shapes = [jax.ShapeDtypeStruct((DOCS_DEV + 16, FEAT), jnp.bfloat16)] * QUERIES
    else:
        shapes = [
            jax.ShapeDtypeStruct((docs, FEAT), jnp.float32),
            jax.ShapeDtypeStruct((docs, BLOCK), jnp.float32),
        ]
    return pl.pallas_call(
        functools.partial(smooth_kernel, len(queries), len(cands), own, first_cands, last),
        in_specs=[smem] + [free] * (len(queries) + len(cands)) + [hbm] * (2 if last else 0),
        out_specs=[vmem if last else hbm] * len(shapes),
        out_shape=shapes,
        scratch_shapes=[
            pltpu.VMEM((docs, FEAT), jnp.float32),
            pltpu.VMEM((docs, BLOCK), jnp.float32),
            pltpu.VMEM((docs, EMB), jnp.bfloat16),
            pltpu.VMEM((len(cands) * DOCS_DEV, EMB + FEAT), jnp.bfloat16),
            pltpu.SemaphoreType.DMA((3 + len(queries) + len(cands),)),
        ],
        compiler_params=small(28),
        cost_estimate=pl.CostEstimate(
            flops=40 * 2 * BLOCK * BLOCK * (EMB + FEAT),
            bytes_accessed=sum(2 * v.size for v in (*queries, *cands)),
            transcendentals=40 * BLOCK * BLOCK,
        ),
        name="smooth_late" if last else "smooth_early",
    )(*operands)


def combine_kernel(*refs):
    parts, out = refs[:-1], refs[-1]
    top = parts[0][pl.ds(0, DOCS_DEV), :].astype(jnp.float32)
    sums = parts[0][pl.ds(DOCS_DEV, 16), :].astype(jnp.float32)
    for part in parts[1:]:
        top += part[pl.ds(0, DOCS_DEV), :].astype(jnp.float32)
        sums += part[pl.ds(DOCS_DEV, 16), :].astype(jnp.float32)
    bottom = sums[0:1, :] + sums[8:9, :]
    diagonal = lax.broadcasted_iota(jnp.int32, (BLOCK, BLOCK), 0) == lax.broadcasted_iota(
        jnp.int32, (BLOCK, BLOCK), 1
    )
    for b in range(NB_DEV):
        line = jnp.broadcast_to(bottom[:, b * BLOCK : (b + 1) * BLOCK], (BLOCK, BLOCK))
        column = jnp.sum(jnp.where(diagonal, line, 0.0), axis=1, keepdims=True)
        out[pl.ds(b * BLOCK, BLOCK), :] = (top[b * BLOCK : (b + 1) * BLOCK] / column).astype(jnp.bfloat16)


def steps(embeddings, features, candidates):
    partner_lists = send(candidates, y_of=partner_a)
    cand = cand_payload(embeddings, features)
    units = query_payload(cand, candidates, partner_lists)

    c_o, c_b = send(cand, dz=2), send(cand, y_of=partner_b)
    c_r, c_l = send(cand, dz=1), send(cand, dz=-1)
    c_br, c_bl = send(c_b, dz=1), send(c_b, dz=-1)
    c_bo = send(c_o, y_of=partner_b)
    q_r, q_l = send(units, dx=1), send(units, dx=-1)
    q_a, q_o = send(units, y_of=partner_a), send(units, dx=2)
    q_ar, q_al = send(q_a, dx=1), send(q_a, dx=-1)
    q_ao = send(q_o, y_of=partner_a)

    q_early, q_late = [q_r, q_l, q_a, q_o], [q_ar, q_al, q_ao]
    early, late = [cand, c_b, c_o, c_r, c_l, c_bo], [c_br, c_bl]
    early_other = [send(c, flip_core=True) for c in early]
    late_other = [send(c, flip_core=True) for c in late]

    codes = pair_codes(candidates, partner_lists, q_r, q_l, q_o)
    state = smooth(codes, q_early, early + early_other, 0, len(early), None)
    payloads = smooth(
        codes,
        q_early + q_late,
        late + late_other + early + early_other,
        2 * len(late),
        2 * len(late),
        state,
    )
    home = [
        dict(dx=-1), dict(dx=1), dict(y_of=partner_a), dict(dx=2),
        dict(dx=-1, y_of=partner_a), dict(dx=1, y_of=partner_a), dict(dx=2, y_of=partner_a),
    ]
    order = [6, 2, 4, 5, 3, 0, 1]
    back = [send(payloads[1 + i], **home[i]) for i in order]
    return pl.pallas_call(
        combine_kernel,
        in_specs=[pl.BlockSpec(memory_space=pltpu.VMEM)] * (1 + len(back)),
        out_shape=jax.ShapeDtypeStruct((DOCS_DEV, FEAT), jnp.bfloat16),
        compiler_params=pltpu.CompilerParams(vmem_limit_bytes=8 << 20),
        name="combine",
    )(payloads[0], *back)


def solution(mesh):
    spec = P(("row", "col"), None)
    return jax.shard_map(steps, mesh=mesh, in_specs=(spec, spec, spec), out_specs=spec, check_vma=False)
```

time: 417 us -> 122 us (0.29)
  blocking collectives: 229 us -> 0 us
  waiting for transfers between devices: 101 us -> 54.9 us
  starting transfers between devices: 0.12 us -> 38.7 us
  local copies, waits for them, and re-layouts: 33 us -> 1.25 us
  matrix products: 29.2 us -> 0 us
  Pallas kernels: 0 us -> 26.6 us
  between operations: 13.9 us -> 0.11 us
  other arithmetic: 7.67 us -> 0 us
    unnamed x1 -> x0, blocking collectives: 204 us -> none
    all_gather x3 -> x0, waiting for transfers between devices: 89 us -> none  [the longest x1 73.1 us: on_device(): query_flat = lax.all_gather(units, 'col', axis=0, tiled=True)]
    ppermute x0 -> x30, waiting for transfers between devices: none -> 54.9 us  [send(): return lax.ppermute(value, AXES, hop(**where))]
    ppermute x0 -> x30, starting transfers between devices: none -> 38.7 us  [send(): return lax.ppermute(value, AXES, hop(**where))]
    dot_general x4 -> x0, matrix products: 29.2 us -> none  [the longest x2 18.6 us: turn(): jnp.einsum('qie,qje->qij', query_units, cand_blk, preferred_element_type=...]
    pallas_call x0 -> x6, Pallas kernels: none -> 26.6 us  [the longest x2 20.8 us: smooth(): pl.pallas_call(functools.partial(smooth_kernel, len(queries), len(cands),...]
    all_gather x1 -> x0, blocking collectives: 25 us -> none  [on_device(): block_lists = lax.all_gather(candidates, 'col', axis=0, tiled=True)]
    gather x4 -> x0, local copies, waits for them, and re-layouts: 15.7 us -> none  [the longest x2 14.4 us: turn(): cand_blk = jnp.take(cand_units, cand_idx, axis=0)]
  transfers between devices with their start and end apart: 4 -> 30, of which waited for: 3 -> 15; matrix products, arithmetic and copies ran while one was open for 5% -> 0% of each run, Pallas kernels for 0% -> 9%
where the time goes in v1:
time: 122 us
  waiting for transfers between devices  54.9 us (45%)
  starting transfers between devices  38.7 us (32%)
  Pallas kernels  26.6 us (22%)
  local copies, waits for them, and re-layouts  1.25 us (1%)
    ppermute x30, waiting for transfers between devices, send(): return lax.ppermute(value, AXES, hop(**where))  54.9 us
    ppermute x30, starting transfers between devices, send(): return lax.ppermute(value, AXES, hop(**where))  38.7 us
    pallas_call x2, Pallas kernels, smooth(): pl.pallas_call(functools.partial(smooth_kernel, len(queries), len(cands),...  20.8 us
  transfers between devices with their start and end apart: 30, of which 15 were waited for; matrix products, arithmetic and copies ran while one was open for 0% of the time, Pallas kernels for 9%

profile of v1, /device:TPU:0, one launch (start us, length us, event | category | flops | bytes accessed | tf_op | source)
XLA Modules:
  0.0 121.6 jit_solution(14486481387833613847)
XLA Ops:
  0.0 1.7 %collective-permute-start = (s32[2,38]{1,0:T(2,128)}, s32[2,38]{1,0:T(2,128)S(1)}, u32[]{:S(2)}, u32[]{:S(2)}) collective-permute-start(s32[2,38]{1,0:T(2,128)} %own_ref.3), channel_id=1, source_target_pairs={{0,1},{1,0},{2,3},{3,2},{4,5},{5,4},{6,7},{7,6},{8,9},{9,8},{10,11... | collective-permute-start | bytes 920 | tf_op jit(solution)/shard_map/ppermute | solution.py:42
  1.7 2.1 %cand.1.unit_ref.refs_5_.refs_12_ = bf16[256,1280]{1,0:T(8,128)(2,1)} custom-call(bf16[256,1024]{1,0:T(8,128)(2,1)} %emb_ref.1, bf16[256,256]{1,0:T(8,128)(2,1)} %feat_ref.1), custom_call_target="tpu_custom_call" | custom-call | tf_op jit(solution)/shard_map/cand/pallas_call | solution.py:67
  4.4 1.9 %query.1 = bf16[272,1024]{1,0:T(8,128)(2,1)} custom-call(bf16[256,1280]{1,0:T(8,128)(2,1)} %cand.1.unit_ref.refs_5_.refs_12_, s32[2,38]{1,0:T(2,128)} %own_ref.3, s32[2,38]{1,0:T(2,128)} %copy-done.2), custom_call_target="tpu_custom_call" | custom-call | tf_op jit(solution)/shard_map/query/pallas_call | solution.py:75
  6.3 1.7 %collective-permute-start.4 = (bf16[272,1024]{1,0:T(8,128)(2,1)}, bf16[272,1024]{1,0:T(8,128)(2,1)S(1)}, u32[]{:S(2)}, u32[]{:S(2)}) collective-permute-start(bf16[272,1024]{1,0:T(8,128)(2,1)} %query.1), channel_id=1, source_target_pairs={{0,1},{1,0},{2,3},{3,2},{4,5},{5,4},{6,7},{7,6},{8,9},{9,8},{10,11... | collective-permute-start | bytes 1671176 | tf_op jit(solution)/shard_map/ppermute | solution.py:42
  8.0 3.0 %collective-permute-start.3 = (bf16[272,1024]{1,0:T(8,128)(2,1)}, bf16[272,1024]{1,0:T(8,128)(2,1)S(1)}, u32[]{:S(2)}, u32[]{:S(2)}) collective-permute-start(bf16[272,1024]{1,0:T(8,128)(2,1)} %query.1), channel_id=1, source_target_pairs={{0,64},{1,65},{2,66},{3,67},{4,68},{5,69},{6,70},{7,71},{8,72},{9,... | collective-permute-start | bytes 1671176 | tf_op jit(solution)/shard_map/ppermute | solution.py:42
  11.0 4.0 %collective-permute-start.15 = (bf16[256,1280]{1,0:T(8,128)(2,1)}, bf16[256,1280]{1,0:T(8,128)(2,1)S(1)}, u32[]{:S(2)}, u32[]{:S(2)}) collective-permute-start(bf16[256,1280]{1,0:T(8,128)(2,1)} %cand.1.unit_ref.refs_5_.refs_12_), channel_id=1, source_target_pairs={{0,12},{1,13},{2,14},{3,15},{4,0},{5,1},{6,2},{7,3},{8,4},{9,5},{1... | collective-permute-start | bytes 1966088 | tf_op jit(solution)/shard_map/ppermute | solution.py:42
  15.0 1.9 %collective-permute-start.13 = (bf16[256,1280]{1,0:T(8,128)(2,1)}, bf16[256,1280]{1,0:T(8,128)(2,1)S(1)}, u32[]{:S(2)}, u32[]{:S(2)}) collective-permute-start(bf16[256,1280]{1,0:T(8,128)(2,1)} %cand.1.unit_ref.refs_5_.refs_12_), channel_id=1, source_target_pairs={{0,8},{1,9},{2,10},{3,11},{4,12},{5,13},{6,14},{7,15},{8,0},{9,1},... | collective-permute-start | bytes 1966088 | tf_op jit(solution)/shard_map/ppermute | solution.py:42
  16.9 3.7 %collective-permute-done.4.refs_3_ = bf16[272,1024]{1,0:T(8,128)(2,1)S(1)} collective-permute-done((bf16[272,1024]{1,0:T(8,128)(2,1)}, bf16[272,1024]{1,0:T(8,128)(2,1)S(1)}, u32[]{:S(2)}, u32[]{:S(2)}) %collective-permute-start.4) | collective-permute-done | bytes 557088 | tf_op jit(solution)/shard_map/ppermute | solution.py:42
  20.6 2.8 %collective-permute-start.2 = (bf16[272,1024]{1,0:T(8,128)(2,1)}, bf16[272,1024]{1,0:T(8,128)(2,1)S(1)}, u32[]{:S(2)}, u32[]{:S(2)}) collective-permute-start(bf16[272,1024]{1,0:T(8,128)(2,1)} %query.1), channel_id=1, source_target_pairs={{0,96},{1,97},{2,98},{3,99},{4,100},{5,101},{6,102},{7,103},{8,104... | collective-permute-start | bytes 1671176 | tf_op jit(solution)/shard_map/ppermute | solution.py:42
  23.3 0.8 collective-permute-start.1
  24.2 10.5 %collective-permute-done.2.l_ref.refs_2_ = bf16[272,1024]{1,0:T(8,128)(2,1)S(1)} collective-permute-done((bf16[272,1024]{1,0:T(8,128)(2,1)}, bf16[272,1024]{1,0:T(8,128)(2,1)S(1)}, u32[]{:S(2)}, u32[]{:S(2)}) %collective-permute-start.2) | collective-permute-done | bytes 557088 | tf_op jit(solution)/shard_map/ppermute | solution.py:42
  34.6 2.6 %collective-permute-start.8 = (bf16[256,1280]{1,0:T(8,128)(2,1)}, bf16[256,1280]{1,0:T(8,128)(2,1)S(1)}, u32[]{:S(2)}, u32[]{:S(2)}) collective-permute-start(bf16[256,1280]{1,0:T(8,128)(2,1)} %cand.1.unit_ref.refs_5_.refs_12_), channel_id=1, source_target_pairs={{0,3},{1,2},{2,1},{3,0},{4,7},{5,6},{6,5},{7,4},{8,11},{9,10},{10,... | collective-permute-start | bytes 1966088 | tf_op jit(solution)/shard_map/ppermute | solution.py:42
  37.6 4.1 %collective-permute-done.15.refs_9_.refs_16_ = bf16[256,1280]{1,0:T(8,128)(2,1)S(1)} collective-permute-done((bf16[256,1280]{1,0:T(8,128)(2,1)}, bf16[256,1280]{1,0:T(8,128)(2,1)S(1)}, u32[]{:S(2)}, u32[]{:S(2)}) %collective-permute-start.15) | collective-permute-done | bytes 655392 | tf_op jit(solution)/shard_map/ppermute | solution.py:42
  41.7 3.3 %collective-permute-done.14.refs_8_.refs_15_ = bf16[256,1280]{1,0:T(8,128)(2,1)S(1)} collective-permute-done((bf16[256,1280]{1,0:T(8,128)(2,1)}, bf16[256,1280]{1,0:T(8,128)(2,1)S(1)}, u32[]{:S(2)}, u32[]{:S(2)}) %collective-permute-start.14) | collective-permute-done | bytes 655392 | tf_op jit(solution)/shard_map/ppermute | solution.py:42
  45.0 2.6 %collective-permute-start.16 = (bf16[256,1280]{1,0:T(8,128)(2,1)S(1)}, bf16[256,1280]{1,0:T(8,128)(2,1)S(1)}, u32[]{:S(2)}, u32[]{:S(2)}) collective-permute-start(bf16[256,1280]{1,0:T(8,128)(2,1)S(1)} %collective-permute-done.13.refs_7_.refs_14_), channel_id=1, source_target_pairs={{0,3},{1,2},{2,1},{3,0},{4,7},{5,6},{6,5},{7,4},{8,11},{9,10},{10,... | collective-permute-start | bytes 1966088 | tf_op jit(solution)/shard_map/ppermute | solution.py:42
  47.6 5.4 %collective-permute-done.8.refs_6_.refs_13_ = bf16[256,1280]{1,0:T(8,128)(2,1)S(1)} collective-permute-done((bf16[256,1280]{1,0:T(8,128)(2,1)}, bf16[256,1280]{1,0:T(8,128)(2,1)S(1)}, u32[]{:S(2)}, u32[]{:S(2)}) %collective-permute-start.8) | collective-permute-done | bytes 655392 | tf_op jit(solution)/shard_map/ppermute | solution.py:42
  53.0 4.7 %collective-permute-start.10 = (bf16[256,1280]{1,0:T(8,128)(2,1)S(1)}, bf16[256,1280]{1,0:T(8,128)(2,1)S(1)}, u32[]{:S(2)}, u32[]{:S(2)}) collective-permute-start(bf16[256,1280]{1,0:T(8,128)(2,1)S(1)} %collective-permute-done.8.refs_6_.refs_13_), channel_id=1, source_target_pairs={{0,12},{1,13},{2,14},{3,15},{4,0},{5,1},{6,2},{7,3},{8,4},{9,5},{1... | collective-permute-start | bytes 1966088 | tf_op jit(solution)/shard_map/ppermute | solution.py:42
  58.3 6.9 %collective-permute-done.16.refs_10_.refs_17_ = bf16[256,1280]{1,0:T(8,128)(2,1)S(1)} collective-permute-done((bf16[256,1280]{1,0:T(8,128)(2,1)S(1)}, bf16[256,1280]{1,0:T(8,128)(2,1)S(1)}, u32[]{:S(2)}, u32[]{:S(2)}) %collective-permute-start.16) | collective-permute-done | bytes 655392 | tf_op jit(solution)/shard_map/ppermute | solution.py:42
  65.2 1.8 %collective-permute-done.10.refs_9_ = bf16[256,1280]{1,0:T(8,128)(2,1)S(1)} collective-permute-done((bf16[256,1280]{1,0:T(8,128)(2,1)S(1)}, bf16[256,1280]{1,0:T(8,128)(2,1)S(1)}, u32[]{:S(2)}, u32[]{:S(2)}) %collective-permute-start.10) | collective-permute-done | bytes 655392 | tf_op jit(solution)/shard_map/ppermute | solution.py:42
  67.0 3.4 %collective-permute-done.9.refs_8_ = bf16[256,1280]{1,0:T(8,128)(2,1)S(1)} collective-permute-done((bf16[256,1280]{1,0:T(8,128)(2,1)S(1)}, bf16[256,1280]{1,0:T(8,128)(2,1)S(1)}, u32[]{:S(2)}, u32[]{:S(2)}) %collective-permute-start.9) | collective-permute-done | bytes 655392 | tf_op jit(solution)/shard_map/ppermute | solution.py:42
  70.4 2.4 %collective-permute-start.6 = (bf16[272,1024]{1,0:T(8,128)(2,1)S(1)}, bf16[272,1024]{1,0:T(8,128)(2,1)S(1)}, u32[]{:S(2)}, u32[]{:S(2)}) collective-permute-start(bf16[272,1024]{1,0:T(8,128)(2,1)S(1)} %collective-permute-done.4.refs_3_), channel_id=1, source_target_pairs={{0,96},{1,97},{2,98},{3,99},{4,100},{5,101},{6,102},{7,103},{8,104... | collective-permute-start | bytes 1671176 | tf_op jit(solution)/shard_map/ppermute | solution.py:42
  73.9 0.9 codes.1.refs_0_
  74.8 8.5 %smooth_early.1 = (f32[1280,256]{1,0:T(8,128)S(1)}, f32[1280,128]{1,0:T(8,128)S(1)}) custom-call(s32[2,384]{1,0:T(2,128)S(1)} %codes.1.refs_0_, bf16[272,1024]{1,0:T(8,128)(2,1)S(1)} %collective-permute-done.1.r_ref.refs_1_, bf16[272,1024]{1,0:T(8,128)(2,1)S(1)} %collective-permute-done.2.l_ref.refs_2_, ...), custom_call_target="tpu_custom_call" | custom-call | flops 1677721600 | bytes 10092544 | tf_op jit(solution)/shard_map/smooth_early/pallas_call | solution.py:316
  83.3 2.1 %collective-permute-done.6.refs_6_ = bf16[272,1024]{1,0:T(8,128)(2,1)S(1)} collective-permute-done((bf16[272,1024]{1,0:T(8,128)(2,1)S(1)}, bf16[272,1024]{1,0:T(8,128)(2,1)S(1)}, u32[]{:S(2)}, u32[]{:S(2)}) %collective-permute-start.6) | collective-permute-done | bytes 557088 | tf_op jit(solution)/shard_map/ppermute | solution.py:42
  85.4 3.4 %collective-permute-done.5.refs_5_ = bf16[272,1024]{1,0:T(8,128)(2,1)S(1)} collective-permute-done((bf16[272,1024]{1,0:T(8,128)(2,1)S(1)}, bf16[272,1024]{1,0:T(8,128)(2,1)S(1)}, u32[]{:S(2)}, u32[]{:S(2)}) %collective-permute-start.5) | collective-permute-done | bytes 557088 | tf_op jit(solution)/shard_map/ppermute | solution.py:42
  88.8 12.3 %smooth_late.1 = (bf16[272,256]{1,0:T(8,128)(2,1)S(1)}, bf16[272,256]{1,0:T(8,128)(2,1)S(1)}, bf16[272,256]{1,0:T(8,128)(2,1)S(1)}, bf16[272,256]{1,0:T(8,128)(2...) custom-call(s32[2,384]{1,0:T(2,128)S(1)} %codes.1.refs_0_, ...), custom_call_target="tpu_custom_call" | custom-call | flops 1677721600 | bytes 14385152 | tf_op jit(solution)/shard_map/smooth_late/pallas_call | solution.py:316
  101.4 2.6 %collective-permute-start.25 = (bf16[272,256]{1,0:T(8,128)(2,1)S(1)}, bf16[272,256]{1,0:T(8,128)(2,1)S(1)}, u32[]{:S(2)}, u32[]{:S(2)}) collective-permute-start(bf16[272,256]{1,0:T(8,128)(2,1)S(1)} %get-tuple-element.20), channel_id=1, source_target_pairs={{0,97},{1,96},{2,99},{3,98},{4,101},{5,100},{6,103},{7,102},{8,105... | collective-permute-start | bytes 417800 | tf_op jit(solution)/shard_map/ppermute | solution.py:42
  104.3 4.8 %collective-permute-start.27 = (bf16[272,256]{1,0:T(8,128)(2,1)S(1)}, bf16[272,256]{1,0:T(8,128)(2,1)S(1)}, u32[]{:S(2)}, u32[]{:S(2)}) collective-permute-start(bf16[272,256]{1,0:T(8,128)(2,1)S(1)} %get-tuple-element.22), channel_id=1, source_target_pairs={{0,64},{1,65},{2,66},{3,67},{4,68},{5,69},{6,70},{7,71},{8,72},{9,... | collective-permute-start | bytes 417800 | tf_op jit(solution)/shard_map/ppermute | solution.py:42
  109.2 2.3 %collective-permute-done.23.refs_1_ = bf16[272,256]{1,0:T(8,128)(2,1)S(1)} collective-permute-done((bf16[272,256]{1,0:T(8,128)(2,1)S(1)}, bf16[272,256]{1,0:T(8,128)(2,1)S(1)}, u32[]{:S(2)}, u32[]{:S(2)}) %collective-permute-start.23) | collective-permute-done | bytes 139296 | tf_op jit(solution)/shard_map/ppermute | solution.py:42
  111.4 3.1 %collective-permute-done.24.refs_2_ = bf16[272,256]{1,0:T(8,128)(2,1)S(1)} collective-permute-done((bf16[272,256]{1,0:T(8,128)(2,1)S(1)}, bf16[272,256]{1,0:T(8,128)(2,1)S(1)}, u32[]{:S(2)}, u32[]{:S(2)}) %collective-permute-start.24) | collective-permute-done | bytes 139296 | tf_op jit(solution)/shard_map/ppermute | solution.py:42
  114.5 1.5 %collective-permute-start.29 = (bf16[272,256]{1,0:T(8,128)(2,1)S(1)}, bf16[272,256]{1,0:T(8,128)(2,1)S(1)}, u32[]{:S(2)}, u32[]{:S(2)}) collective-permute-start(bf16[272,256]{1,0:T(8,128)(2,1)S(1)} %get-tuple-element.24), channel_id=1, source_target_pairs={{0,32},{1,33},{2,34},{3,35},{4,36},{5,37},{6,38},{7,39},{8,40},{9,... | collective-permute-start | bytes 417800 | tf_op jit(solution)/shard_map/ppermute | solution.py:42
  116.5 4.3 %collective-permute-done.29.refs_7_ = bf16[272,256]{1,0:T(8,128)(2,1)S(1)} collective-permute-done((bf16[272,256]{1,0:T(8,128)(2,1)S(1)}, bf16[272,256]{1,0:T(8,128)(2,1)S(1)}, u32[]{:S(2)}, u32[]{:S(2)}) %collective-permute-start.29) | collective-permute-done | bytes 139296 | tf_op jit(solution)/shard_map/ppermute | solution.py:42
  (42 shorter events, 4.4 us)
Async XLA Ops:
  0.0 73.2 %copy-start.1 = (s32[2,38]{1,0:T(2,128)S(1)}, s32[2,38]{1,0:T(2,128)}, u32[]{:S(2)}) copy-start(s32[2,38]{1,0:T(2,128)} %own_ref.3) | copy-start | bytes 916
  0.0 3.8 %collective-permute-start = (s32[2,38]{1,0:T(2,128)}, s32[2,38]{1,0:T(2,128)S(1)}, u32[]{:S(2)}, u32[]{:S(2)}) collective-permute-start(s32[2,38]{1,0:T(2,128)} %own_ref.3), channel_id=1, source_target_pairs={{0,1},{1,0},{2,3},{3,2},{4,5},{5,4},{6,7},{7,6},{8,9},{9,8},{10,11... | collective-permute-start | bytes 920 | tf_op jit(solution)/shard_map/ppermute | solution.py:42
  3.8 71.0 %copy-start = (bf16[256,1280]{1,0:T(8,128)(2,1)S(1)}, bf16[256,1280]{1,0:T(8,128)(2,1)}, u32[]{:S(2)}) copy-start(bf16[256,1280]{1,0:T(8,128)(2,1)} %cand.1.unit_ref.refs_5_.refs_12_) | copy-start | bytes 1966084
  6.3 14.3 %collective-permute-start.4 = (bf16[272,1024]{1,0:T(8,128)(2,1)}, bf16[272,1024]{1,0:T(8,128)(2,1)S(1)}, u32[]{:S(2)}, u32[]{:S(2)}) collective-permute-start(bf16[272,1024]{1,0:T(8,128)(2,1)} %query.1), channel_id=1, source_target_pairs={{0,1},{1,0},{2,3},{3,2},{4,5},{5,4},{6,7},{7,6},{8,9},{9,8},{10,11... | collective-permute-start | bytes 1671176 | tf_op jit(solution)/shard_map/ppermute | solution.py:42
  8.0 15.4 %collective-permute-start.3 = (bf16[272,1024]{1,0:T(8,128)(2,1)}, bf16[272,1024]{1,0:T(8,128)(2,1)S(1)}, u32[]{:S(2)}, u32[]{:S(2)}) collective-permute-start(bf16[272,1024]{1,0:T(8,128)(2,1)} %query.1), channel_id=1, source_target_pairs={{0,64},{1,65},{2,66},{3,67},{4,68},{5,69},{6,70},{7,71},{8,72},{9,... | collective-permute-start | bytes 1671176 | tf_op jit(solution)/shard_map/ppermute | solution.py:42
  11.0 30.7 %collective-permute-start.15 = (bf16[256,1280]{1,0:T(8,128)(2,1)}, bf16[256,1280]{1,0:T(8,128)(2,1)S(1)}, u32[]{:S(2)}, u32[]{:S(2)}) collective-permute-start(bf16[256,1280]{1,0:T(8,128)(2,1)} %cand.1.unit_ref.refs_5_.refs_12_), channel_id=1, source_target_pairs={{0,12},{1,13},{2,14},{3,15},{4,0},{5,1},{6,2},{7,3},{8,4},{9,5},{1... | collective-permute-start | bytes 1966088 | tf_op jit(solution)/shard_map/ppermute | solution.py:42
  15.0 29.9 %collective-permute-start.14 = (bf16[256,1280]{1,0:T(8,128)(2,1)}, bf16[256,1280]{1,0:T(8,128)(2,1)S(1)}, u32[]{:S(2)}, u32[]{:S(2)}) collective-permute-start(bf16[256,1280]{1,0:T(8,128)(2,1)} %cand.1.unit_ref.refs_5_.refs_12_), channel_id=1, source_target_pairs={{0,4},{1,5},{2,6},{3,7},{4,8},{5,9},{6,10},{7,11},{8,12},{9,13},{1... | collective-permute-start | bytes 1966088 | tf_op jit(solution)/shard_map/ppermute | solution.py:42
  15.0 30.0 %collective-permute-start.13 = (bf16[256,1280]{1,0:T(8,128)(2,1)}, bf16[256,1280]{1,0:T(8,128)(2,1)S(1)}, u32[]{:S(2)}, u32[]{:S(2)}) collective-permute-start(bf16[256,1280]{1,0:T(8,128)(2,1)} %cand.1.unit_ref.refs_5_.refs_12_), channel_id=1, source_target_pairs={{0,8},{1,9},{2,10},{3,11},{4,12},{5,13},{6,14},{7,15},{8,0},{9,1},... | collective-permute-start | bytes 1966088 | tf_op jit(solution)/shard_map/ppermute | solution.py:42
  20.6 14.1 %collective-permute-start.2 = (bf16[272,1024]{1,0:T(8,128)(2,1)}, bf16[272,1024]{1,0:T(8,128)(2,1)S(1)}, u32[]{:S(2)}, u32[]{:S(2)}) collective-permute-start(bf16[272,1024]{1,0:T(8,128)(2,1)} %query.1), channel_id=1, source_target_pairs={{0,96},{1,97},{2,98},{3,99},{4,100},{5,101},{6,102},{7,103},{8,104... | collective-permute-start | bytes 1671176 | tf_op jit(solution)/shard_map/ppermute | solution.py:42
  23.3 14.3 %collective-permute-start.1 = (bf16[272,1024]{1,0:T(8,128)(2,1)}, bf16[272,1024]{1,0:T(8,128)(2,1)S(1)}, u32[]{:S(2)}, u32[]{:S(2)}) collective-permute-start(bf16[272,1024]{1,0:T(8,128)(2,1)} %query.1), channel_id=1, source_target_pairs={{0,32},{1,33},{2,34},{3,35},{4,36},{5,37},{6,38},{7,39},{8,40},{9,... | collective-permute-start | bytes 1671176 | tf_op jit(solution)/shard_map/ppermute | solution.py:42
  34.6 18.4 %collective-permute-start.8 = (bf16[256,1280]{1,0:T(8,128)(2,1)}, bf16[256,1280]{1,0:T(8,128)(2,1)S(1)}, u32[]{:S(2)}, u32[]{:S(2)}) collective-permute-start(bf16[256,1280]{1,0:T(8,128)(2,1)} %cand.1.unit_ref.refs_5_.refs_12_), channel_id=1, source_target_pairs={{0,3},{1,2},{2,1},{3,0},{4,7},{5,6},{6,5},{7,4},{8,11},{9,10},{10,... | collective-permute-start | bytes 1966088 | tf_op jit(solution)/shard_map/ppermute | solution.py:42
  37.6 20.1 %collective-permute-start.17 = (bf16[256,1280]{1,0:T(8,128)(2,1)}, bf16[256,1280]{1,0:T(8,128)(2,1)S(1)}, u32[]{:S(2)}, u32[]{:S(2)}) collective-permute-start(bf16[256,1280]{1,0:T(8,128)(2,1)} %cand.1.unit_ref.refs_5_.refs_12_), channel_id=1, source_target_pairs={{0,16},{1,17},{2,18},{3,19},{4,20},{5,21},{6,22},{7,23},{8,24},{9,... | collective-permute-start | bytes 1966088 | tf_op jit(solution)/shard_map/ppermute | solution.py:42
  41.7 16.0 %collective-permute-start.21 = (bf16[256,1280]{1,0:T(8,128)(2,1)S(1)}, bf16[256,1280]{1,0:T(8,128)(2,1)S(1)}, u32[]{:S(2)}, u32[]{:S(2)}) collective-permute-start(bf16[256,1280]{1,0:T(8,128)(2,1)S(1)} %collective-permute-done.15.refs_9_.refs_16_), channel_id=1, source_target_pairs={{0,16},{1,17},{2,18},{3,19},{4,20},{5,21},{6,22},{7,23},{8,24},{9,... | collective-permute-start | bytes 1966088 | tf_op jit(solution)/shard_map/ppermute | solution.py:42
  45.0 12.8 %collective-permute-start.20 = (bf16[256,1280]{1,0:T(8,128)(2,1)S(1)}, bf16[256,1280]{1,0:T(8,128)(2,1)S(1)}, u32[]{:S(2)}, u32[]{:S(2)}) collective-permute-start(bf16[256,1280]{1,0:T(8,128)(2,1)S(1)} %collective-permute-done.14.refs_8_.refs_15_), channel_id=1, source_target_pairs={{0,16},{1,17},{2,18},{3,19},{4,20},{5,21},{6,22},{7,23},{8,24},{9,... | collective-permute-start | bytes 1966088 | tf_op jit(solution)/shard_map/ppermute | solution.py:42
  45.0 20.2 %collective-permute-start.16 = (bf16[256,1280]{1,0:T(8,128)(2,1)S(1)}, bf16[256,1280]{1,0:T(8,128)(2,1)S(1)}, u32[]{:S(2)}, u32[]{:S(2)}) collective-permute-start(bf16[256,1280]{1,0:T(8,128)(2,1)S(1)} %collective-permute-done.13.refs_7_.refs_14_), channel_id=1, source_target_pairs={{0,3},{1,2},{2,1},{3,0},{4,7},{5,6},{6,5},{7,4},{8,11},{9,10},{10,... | collective-permute-start | bytes 1966088 | tf_op jit(solution)/shard_map/ppermute | solution.py:42
  53.0 13.9 %collective-permute-start.10 = (bf16[256,1280]{1,0:T(8,128)(2,1)S(1)}, bf16[256,1280]{1,0:T(8,128)(2,1)S(1)}, u32[]{:S(2)}, u32[]{:S(2)}) collective-permute-start(bf16[256,1280]{1,0:T(8,128)(2,1)S(1)} %collective-permute-done.8.refs_6_.refs_13_), channel_id=1, source_target_pairs={{0,12},{1,13},{2,14},{3,15},{4,0},{5,1},{6,2},{7,3},{8,4},{9,5},{1... | collective-permute-start | bytes 1966088 | tf_op jit(solution)/shard_map/ppermute | solution.py:42
  57.7 12.7 %collective-permute-start.9 = (bf16[256,1280]{1,0:T(8,128)(2,1)S(1)}, bf16[256,1280]{1,0:T(8,128)(2,1)S(1)}, u32[]{:S(2)}, u32[]{:S(2)}) collective-permute-start(bf16[256,1280]{1,0:T(8,128)(2,1)S(1)} %collective-permute-done.8.refs_6_.refs_13_), channel_id=1, source_target_pairs={{0,4},{1,5},{2,6},{3,7},{4,8},{5,9},{6,10},{7,11},{8,12},{9,13},{1... | collective-permute-start | bytes 1966088 | tf_op jit(solution)/shard_map/ppermute | solution.py:42
  57.7 12.7 %collective-permute-start.19 = (bf16[256,1280]{1,0:T(8,128)(2,1)S(1)}, bf16[256,1280]{1,0:T(8,128)(2,1)S(1)}, u32[]{:S(2)}, u32[]{:S(2)}) collective-permute-start(bf16[256,1280]{1,0:T(8,128)(2,1)S(1)} %collective-permute-done.13.refs_7_.refs_14_), channel_id=1, source_target_pairs={{0,16},{1,17},{2,18},{3,19},{4,20},{5,21},{6,22},{7,23},{8,24},{9,... | collective-permute-start | bytes 1966088 | tf_op jit(solution)/shard_map/ppermute | solution.py:42
  57.8 15.0 %collective-permute-start.18 = (bf16[256,1280]{1,0:T(8,128)(2,1)S(1)}, bf16[256,1280]{1,0:T(8,128)(2,1)S(1)}, u32[]{:S(2)}, u32[]{:S(2)}) collective-permute-start(bf16[256,1280]{1,0:T(8,128)(2,1)S(1)} %collective-permute-done.8.refs_6_.refs_13_), channel_id=1, source_target_pairs={{0,16},{1,17},{2,18},{3,19},{4,20},{5,21},{6,22},{7,23},{8,24},{9,... | collective-permute-start | bytes 1966088 | tf_op jit(solution)/shard_map/ppermute | solution.py:42
  65.2 7.6 %collective-permute-start.22 = (bf16[256,1280]{1,0:T(8,128)(2,1)S(1)}, bf16[256,1280]{1,0:T(8,128)(2,1)S(1)}, u32[]{:S(2)}, u32[]{:S(2)}) collective-permute-start(bf16[256,1280]{1,0:T(8,128)(2,1)S(1)} %collective-permute-done.16.refs_10_.refs_17_), channel_id=1, source_target_pairs={{0,16},{1,17},{2,18},{3,19},{4,20},{5,21},{6,22},{7,23},{8,24},{9,... | collective-permute-start | bytes 1966088 | tf_op jit(solution)/shard_map/ppermute | solution.py:42
  67.0 21.8 %collective-permute-start.12 = (bf16[256,1280]{1,0:T(8,128)(2,1)S(1)}, bf16[256,1280]{1,0:T(8,128)(2,1)S(1)}, u32[]{:S(2)}, u32[]{:S(2)}) collective-permute-start(bf16[256,1280]{1,0:T(8,128)(2,1)S(1)} %collective-permute-done.10.refs_9_), channel_id=1, source_target_pairs={{0,16},{1,17},{2,18},{3,19},{4,20},{5,21},{6,22},{7,23},{8,24},{9,... | collective-permute-start | bytes 1966088 | tf_op jit(solution)/shard_map/ppermute | solution.py:42
  70.4 18.4 %collective-permute-start.11 = (bf16[256,1280]{1,0:T(8,128)(2,1)S(1)}, bf16[256,1280]{1,0:T(8,128)(2,1)S(1)}, u32[]{:S(2)}, u32[]{:S(2)}) collective-permute-start(bf16[256,1280]{1,0:T(8,128)(2,1)S(1)} %collective-permute-done.9.refs_8_), channel_id=1, source_target_pairs={{0,16},{1,17},{2,18},{3,19},{4,20},{5,21},{6,22},{7,23},{8,24},{9,... | collective-permute-start | bytes 1966088 | tf_op jit(solution)/shard_map/ppermute | solution.py:42
  70.4 15.0 %collective-permute-start.6 = (bf16[272,1024]{1,0:T(8,128)(2,1)S(1)}, bf16[272,1024]{1,0:T(8,128)(2,1)S(1)}, u32[]{:S(2)}, u32[]{:S(2)}) collective-permute-start(bf16[272,1024]{1,0:T(8,128)(2,1)S(1)} %collective-permute-done.4.refs_3_), channel_id=1, source_target_pairs={{0,96},{1,97},{2,98},{3,99},{4,100},{5,101},{6,102},{7,103},{8,104... | collective-permute-start | bytes 1671176 | tf_op jit(solution)/shard_map/ppermute | solution.py:42
  72.8 16.0 %collective-permute-start.5 = (bf16[272,1024]{1,0:T(8,128)(2,1)S(1)}, bf16[272,1024]{1,0:T(8,128)(2,1)S(1)}, u32[]{:S(2)}, u32[]{:S(2)}) collective-permute-start(bf16[272,1024]{1,0:T(8,128)(2,1)S(1)} %collective-permute-done.4.refs_3_), channel_id=1, source_target_pairs={{0,32},{1,33},{2,34},{3,35},{4,36},{5,37},{6,38},{7,39},{8,40},{9,... | collective-permute-start | bytes 1671176 | tf_op jit(solution)/shard_map/ppermute | solution.py:42
  72.8 16.0 %collective-permute-start.7 = (bf16[272,1024]{1,0:T(8,128)(2,1)S(1)}, bf16[272,1024]{1,0:T(8,128)(2,1)S(1)}, u32[]{:S(2)}, u32[]{:S(2)}) collective-permute-start(bf16[272,1024]{1,0:T(8,128)(2,1)S(1)} %collective-permute-done.3.o_ref.refs_4_), channel_id=1, source_target_pairs={{0,1},{1,0},{2,3},{3,2},{4,5},{5,4},{6,7},{7,6},{8,9},{9,8},{10,11... | collective-permute-start | bytes 1671176 | tf_op jit(solution)/shard_map/ppermute | solution.py:42
  101.2 10.3 %collective-permute-start.23 = (bf16[272,256]{1,0:T(8,128)(2,1)S(1)}, bf16[272,256]{1,0:T(8,128)(2,1)S(1)}, u32[]{:S(2)}, u32[]{:S(2)}) collective-permute-start(bf16[272,256]{1,0:T(8,128)(2,1)S(1)} %get-tuple-element.18), channel_id=1, source_target_pairs={{0,65},{1,64},{2,67},{3,66},{4,69},{5,68},{6,71},{7,70},{8,73},{9,... | collective-permute-start | bytes 417800 | tf_op jit(solution)/shard_map/ppermute | solution.py:42
  101.3 13.2 %collective-permute-start.24 = (bf16[272,256]{1,0:T(8,128)(2,1)S(1)}, bf16[272,256]{1,0:T(8,128)(2,1)S(1)}, u32[]{:S(2)}, u32[]{:S(2)}) collective-permute-start(bf16[272,256]{1,0:T(8,128)(2,1)S(1)} %get-tuple-element.19), channel_id=1, source_target_pairs={{0,1},{1,0},{2,3},{3,2},{4,5},{5,4},{6,7},{7,6},{8,9},{9,8},{10,11... | collective-permute-start | bytes 417800 | tf_op jit(solution)/shard_map/ppermute | solution.py:42
  101.4 14.6 %collective-permute-start.25 = (bf16[272,256]{1,0:T(8,128)(2,1)S(1)}, bf16[272,256]{1,0:T(8,128)(2,1)S(1)}, u32[]{:S(2)}, u32[]{:S(2)}) collective-permute-start(bf16[272,256]{1,0:T(8,128)(2,1)S(1)} %get-tuple-element.20), channel_id=1, source_target_pairs={{0,97},{1,96},{2,99},{3,98},{4,101},{5,100},{6,103},{7,102},{8,105... | collective-permute-start | bytes 417800 | tf_op jit(solution)/shard_map/ppermute | solution.py:42
  104.0 12.0 %collective-permute-start.26 = (bf16[272,256]{1,0:T(8,128)(2,1)S(1)}, bf16[272,256]{1,0:T(8,128)(2,1)S(1)}, u32[]{:S(2)}, u32[]{:S(2)}) collective-permute-start(bf16[272,256]{1,0:T(8,128)(2,1)S(1)} %get-tuple-element.21), channel_id=1, source_target_pairs={{0,33},{1,32},{2,35},{3,34},{4,37},{5,36},{6,39},{7,38},{8,41},{9,... | collective-permute-start | bytes 417800 | tf_op jit(solution)/shard_map/ppermute | solution.py:42
  104.3 11.6 %collective-permute-start.27 = (bf16[272,256]{1,0:T(8,128)(2,1)S(1)}, bf16[272,256]{1,0:T(8,128)(2,1)S(1)}, u32[]{:S(2)}, u32[]{:S(2)}) collective-permute-start(bf16[272,256]{1,0:T(8,128)(2,1)S(1)} %get-tuple-element.22), channel_id=1, source_target_pairs={{0,64},{1,65},{2,66},{3,67},{4,68},{5,69},{6,70},{7,71},{8,72},{9,... | collective-permute-start | bytes 417800 | tf_op jit(solution)/shard_map/ppermute | solution.py:42
  111.4 5.1 %collective-permute-start.28 = (bf16[272,256]{1,0:T(8,128)(2,1)S(1)}, bf16[272,256]{1,0:T(8,128)(2,1)S(1)}, u32[]{:S(2)}, u32[]{:S(2)}) collective-permute-start(bf16[272,256]{1,0:T(8,128)(2,1)S(1)} %get-tuple-element.23), channel_id=1, source_target_pairs={{0,96},{1,97},{2,98},{3,99},{4,100},{5,101},{6,102},{7,103},{8,104... | collective-permute-start | bytes 417800 | tf_op jit(solution)/shard_map/ppermute | solution.py:42
  114.5 6.3 %collective-permute-start.29 = (bf16[272,256]{1,0:T(8,128)(2,1)S(1)}, bf16[272,256]{1,0:T(8,128)(2,1)S(1)}, u32[]{:S(2)}, u32[]{:S(2)}) collective-permute-start(bf16[272,256]{1,0:T(8,128)(2,1)S(1)} %get-tuple-element.24), channel_id=1, source_target_pairs={{0,32},{1,33},{2,34},{3,35},{4,36},{5,37},{6,38},{7,39},{8,40},{9,... | collective-permute-start | bytes 417800 | tf_op jit(solution)/shard_map/ppermute | solution.py:42
  (2 other events, 1.2 us)
